TPU v7x, 32 devices: a whole 2x2x4 slice. The times are simulated.
32 devices in a mesh: dp: 8 (over z, y), mp: 4 (over x, core).
Axes of the slice: x: 2, y: 2, z: 4, core: 2. Of those that a mesh axis runs over, the one named last changes fastest.
Arguments:
- hidden: bfloat16 [16384, 768], P('dp'), may hold values from -6 to 6
- upstream: bfloat16 [16384, 768], P('dp'), may hold values from -3 to 3
- segment_ids: int32 [16384], P('dp'), may hold values from 0 to 16, as said below
- cls_positions: int32 [16, 16], P('dp'), may hold values from 0 to 872, as said below
- positives: int32 [128], replicated, may hold values from 0 to 127, each once
- w_query: bfloat16 [768, 768], P(None, 'mp'), may hold values from -0.21875 to 0.21875
- b_query: float32 [768], P('mp'), may hold values from -3 to 3
- w_key: bfloat16 [768, 768], P(None, 'mp'), may hold values from -0.21875 to 0.21875
- w_value: bfloat16 [768, 768], P(None, 'mp'), may hold values from -0.21875 to 0.21875
- b_value: float32 [768], P('mp'), may hold values from -3 to 3
- w_out: bfloat16 [768, 768], P('mp'), may hold values from -1.25 to 1.25
- b_out: float32 [768], replicated, may hold values from -2.5 to 2.5
- gain_attn: float32 [768], replicated, may hold values from 0.5 to 1.5
- shift_attn: float32 [768], replicated, may hold values from -2.5 to 2.5
- w_inner: bfloat16 [768, 3072], P(None, 'mp'), may hold values from -0.21875 to 0.21875
- b_inner: float32 [3072], P('mp'), may hold values from -3 to 3
- w_outer: bfloat16 [3072, 768], P('mp'), may hold values from -0.109375 to 0.109375
- b_outer: float32 [768], replicated, may hold values from -2.5 to 2.5
- gain_final: float32 [768], replicated, may hold values from 0.5 to 1.5
- shift_final: float32 [768], replicated, may hold values from -2.5 to 2.5
Outputs:
- mean_loss: float32 [1], replicated
- layer_out: bfloat16 [16384, 768], P('dp')
- grad_hidden: float32 [16384, 768], P('dp')
- grad_w_query: float32 [768, 768], P(None, 'mp')
- grad_b_query: float32 [768], P('mp')
- grad_w_key: float32 [768, 768], P(None, 'mp')
- grad_w_value: float32 [768, 768], P(None, 'mp')
- grad_b_value: float32 [768], P('mp')
- grad_w_out: float32 [768, 768], P('mp')
- grad_b_out: float32 [768], replicated
- grad_gain_attn: float32 [768], replicated
- grad_shift_attn: float32 [768], replicated
- grad_w_inner: float32 [768, 3072], P(None, 'mp')
- grad_b_inner: float32 [3072], P('mp')
- grad_w_outer: float32 [3072, 768], P('mp')
- grad_b_outer: float32 [768], replicated
- grad_gain_final: float32 [768], replicated
- grad_shift_final: float32 [768], replicated
Inputs may be any that keep to these rules, and one draw needn't show every extreme that they name: `segment_ids`: each packed row of 1024 tokens holds 16 consecutive segments numbered 0 to 15 in order, even numbers queries and odd numbers passages, then padding tokens numbered 2 * 8, of which every row has some. `cls_positions`: entry j < 8 of row r is the first position within the row of segment 2 j, entry 8 + j that of segment 2 j + 1, as given by segment_ids. `positives`: every passage is the positive of exactly one query.
All inputs are finite; a program needn't handle non-finite values.
Results may differ from a plain program's by a relative error of at most 0.013.
Values may be sent and summed in bfloat16 or wider, within the bound.
A program may use at most 128 MiB of HBM per device.

v0:
```python
from functools import partial
import math
import jax
import jax.numpy as jnp
from jax import lax
from jax.sharding import PartitionSpec as P

D = 768
HEAD_DIM = 64
LEN = 1024
PAIRS = 8


def contract_rows(left_arr, right_arr):
    return lax.dot_general(
        left_arr, right_arr, (((0,), (0,)), ((), ())), preferred_element_type=jnp.float32
    )


def contract_cols(left_arr, right_arr):
    return lax.dot_general(
        left_arr, right_arr, (((1,), (1,)), ((), ())), preferred_element_type=jnp.float32
    )


def norm_forward(summed, gain_vec, offset_vec):
    centre = summed - jnp.mean(summed, axis=-1, keepdims=True)
    inverse = lax.rsqrt(jnp.mean(centre * centre, axis=-1, keepdims=True) + 1e-12)
    normed = centre * inverse
    return (normed * gain_vec + offset_vec, normed, inverse)


def norm_backward(grad_rows, normed, inverse, gain_vec):
    scaled = grad_rows * gain_vec
    grad_in = inverse * (
        scaled
        - jnp.mean(scaled, axis=-1, keepdims=True)
        - normed * jnp.mean(scaled * normed, axis=-1, keepdims=True)
    )
    return (grad_in, jnp.sum(grad_rows * normed, axis=0), jnp.sum(grad_rows, axis=0))


def soft_rows(logits, targets, logit_scale):
    largest = jnp.max(logits, axis=-1, keepdims=True)
    expo_rows = jnp.exp(logits - largest)
    totals = jnp.sum(expo_rows, axis=-1, keepdims=True)
    target_hit = targets[:, None] == jnp.arange(logits.shape[1], dtype=jnp.int32)[None, :]
    cross_ent = (
        largest[:, 0] + jnp.log(totals[:, 0]) - jnp.sum(jnp.where(target_hit, logits, 0.0), axis=-1)
    )
    logit_grad = (expo_rows / totals - target_hit.astype(jnp.float32)) * logit_scale
    return (cross_ent, logit_grad)


def on_device(
    hidden,
    upstream,
    segment_ids,
    cls_positions,
    positives,
    w_query,
    b_query,
    w_key,
    w_value,
    b_value,
    w_out,
    b_out,
    gain_attn,
    shift_attn,
    w_inner,
    b_inner,
    w_outer,
    b_outer,
    gain_final,
    shift_final,
):
    highest = lax.Precision.HIGHEST
    token_count = hidden.shape[0]
    row_count = token_count // LEN
    local_width = w_query.shape[1]
    head_count = local_width // HEAD_DIM
    head_scale = 1.0 / math.sqrt(HEAD_DIM)
    logit_scale = 3.0 / math.sqrt(D)
    block_rows = min(512, LEN)
    per_row = LEN // block_rows
    block_count = token_count // block_rows
    query_rows = (
        (jnp.dot(hidden, w_query, preferred_element_type=jnp.float32) + b_query) * head_scale
    ).astype(jnp.bfloat16)
    key_rows = jnp.dot(hidden, w_key, preferred_element_type=jnp.float32).astype(jnp.bfloat16)
    value_rows = (jnp.dot(hidden, w_value, preferred_element_type=jnp.float32) + b_value).astype(
        jnp.bfloat16
    )
    query_blocks = query_rows.reshape(block_count, block_rows, head_count, HEAD_DIM)
    key_seqs = key_rows.reshape(row_count, LEN, head_count, HEAD_DIM)
    value_seqs = value_rows.reshape(row_count, LEN, head_count, HEAD_DIM)
    segment_blocks = segment_ids.reshape(block_count, block_rows)
    segment_seqs = segment_ids.reshape(row_count, LEN)

    def block_scores(block_index):
        row_index = block_index // per_row
        query_block = query_blocks[block_index]
        key_block = key_seqs[row_index]
        scores = jnp.einsum(
            "qhd,khd->hqk", query_block, key_block, preferred_element_type=jnp.float32
        )
        same_doc = segment_blocks[block_index][:, None] == segment_seqs[row_index][None, :]
        return (jnp.where(same_doc[None, :, :], scores, -1e30), row_index, query_block, key_block)

    def forward_block(block_index):
        scores, row_index, query_block, key_block = block_scores(block_index)
        largest = jnp.max(scores, axis=-1, keepdims=True)
        expo_rows = jnp.exp(scores - largest)
        totals = jnp.sum(expo_rows, axis=-1, keepdims=True)
        weights = (expo_rows / totals).astype(jnp.bfloat16)
        context_block = jnp.einsum(
            "hqk,khd->qhd", weights, value_seqs[row_index], preferred_element_type=jnp.float32
        )
        return (context_block.astype(jnp.bfloat16), largest + jnp.log(totals))

    context_blocks, log_totals = lax.map(forward_block, jnp.arange(block_count))
    context = context_blocks.reshape(token_count, local_width)
    attention_part = lax.psum(jnp.dot(context, w_out, preferred_element_type=jnp.float32), "mp")
    attention_part = attention_part + b_out
    hidden_part = hidden.astype(jnp.float32)
    middle_part, normed_one, inverse_one = norm_forward(
        hidden_part + attention_part, gain_attn, shift_attn
    )
    middle_low_part = middle_part.astype(jnp.bfloat16)
    pre_act = jnp.dot(middle_low_part, w_inner, preferred_element_type=jnp.float32) + b_inner
    activated, gelu_back = jax.vjp(partial(jax.nn.gelu, approximate=False), pre_act)
    inner_act = activated.astype(jnp.bfloat16)
    feed_part = lax.psum(jnp.dot(inner_act, w_outer, preferred_element_type=jnp.float32), "mp")
    feed_part = feed_part + b_outer
    final_part, normed_two, inverse_two = norm_forward(
        middle_part + feed_part, gain_final, shift_final
    )
    out_part = final_part.astype(jnp.bfloat16)
    own_count = row_count * PAIRS
    row_start = jnp.arange(row_count, dtype=jnp.int32)[:, None] * LEN
    cls_index = jnp.concatenate(
        [
            (row_start + cls_positions[:, :PAIRS]).reshape(-1),
            (row_start + cls_positions[:, PAIRS:]).reshape(-1),
        ]
    )
    selector = cls_index[:, None] == jnp.arange(token_count, dtype=jnp.int32)[None, :]
    picked = jnp.dot(
        selector.astype(jnp.bfloat16), out_part, preferred_element_type=jnp.float32
    ).astype(jnp.bfloat16)
    query_vecs = picked[:own_count]
    passage_vecs = picked[own_count:]
    device = lax.axis_index("dp")
    dp_count = lax.axis_size("dp")
    own_positive = lax.dynamic_slice_in_dim(positives, device * own_count, own_count)
    passage_all = lax.all_gather(passage_vecs, "dp", axis=0, tiled=True)
    logits = contract_cols(query_vecs, passage_all) * logit_scale
    cross_ent, logit_grad = soft_rows(logits, own_positive, logit_scale)
    loss_term = jnp.sum(cross_ent)
    grad_query_vecs = jnp.dot(logit_grad, passage_all.astype(jnp.float32), precision=highest)
    passage_terms = lax.dot_general(
        logit_grad, query_vecs.astype(jnp.float32), (((0,), (0,)), ((), ())), precision=highest
    )
    grad_passage_vecs = lax.psum_scatter(passage_terms, "dp", scatter_dimension=0, tiled=True)
    grad_cls = jnp.concatenate([grad_query_vecs, grad_passage_vecs], axis=0)
    selector_part = selector.astype(jnp.float32)
    grad_final_part = upstream.astype(jnp.float32) + lax.dot_general(
        selector_part, grad_cls, (((0,), (0,)), ((), ())), precision=highest
    )
    grad_two_part, grad_gain_final, grad_shift_final = norm_backward(
        grad_final_part, normed_two, inverse_two, gain_final
    )
    grad_feed_part = grad_two_part.astype(jnp.bfloat16)
    grad_b_outer = jnp.sum(grad_feed_part.astype(jnp.float32), axis=0)
    grad_w_outer = contract_rows(inner_act, grad_feed_part)
    grad_inner = contract_cols(grad_feed_part, w_outer)
    grad_pre = gelu_back(grad_inner)[0].astype(jnp.bfloat16)
    grad_b_inner = jnp.sum(grad_pre.astype(jnp.float32), axis=0)
    grad_w_inner = contract_rows(middle_low_part, grad_pre)
    back_part = lax.psum(contract_cols(grad_pre, w_inner), "mp")
    grad_middle_part = grad_two_part + back_part
    grad_one_part, grad_gain_attn, grad_shift_attn = norm_backward(
        grad_middle_part, normed_one, inverse_one, gain_attn
    )
    grad_attn_part = grad_one_part.astype(jnp.bfloat16)
    grad_b_out = jnp.sum(grad_attn_part.astype(jnp.float32), axis=0)
    grad_w_out = contract_rows(context, grad_attn_part)
    grad_context = contract_cols(grad_attn_part, w_out).astype(jnp.bfloat16)
    grad_context_blocks = grad_context.reshape(block_count, block_rows, head_count, HEAD_DIM)

    def backward_block(carried, block_index):
        grad_keys, grad_values = carried
        scores, row_index, query_block, key_block = block_scores(block_index)
        probs_full = jnp.exp(scores - log_totals[block_index])
        weights = probs_full.astype(jnp.bfloat16)
        grad_ctx_block = grad_context_blocks[block_index]
        grad_probs = jnp.einsum(
            "qhd,khd->hqk",
            grad_ctx_block,
            value_seqs[row_index],
            preferred_element_type=jnp.float32,
        )
        centre = jnp.sum(probs_full * grad_probs, axis=-1, keepdims=True)
        grad_scores = (probs_full * (grad_probs - centre)).astype(jnp.bfloat16)
        grad_query_block = jnp.einsum(
            "hqk,khd->qhd", grad_scores, key_block, preferred_element_type=jnp.float32
        )
        key_update = jnp.einsum(
            "hqk,qhd->khd", grad_scores, query_block, preferred_element_type=jnp.float32
        )
        value_update = jnp.einsum(
            "hqk,qhd->khd", weights, grad_ctx_block, preferred_element_type=jnp.float32
        )
        grad_keys = grad_keys.at[row_index].add(key_update.reshape(LEN, local_width))
        grad_values = grad_values.at[row_index].add(value_update.reshape(LEN, local_width))
        return ((grad_keys, grad_values), grad_query_block.reshape(block_rows, local_width))

    zero_seqs = jnp.zeros((row_count, LEN, local_width), jnp.float32)
    (grad_keys, grad_values), grad_query_blocks = lax.scan(
        backward_block, (zero_seqs, zero_seqs), jnp.arange(block_count)
    )
    grad_query_pre = grad_query_blocks.reshape(token_count, local_width).astype(
        jnp.bfloat16
    ) * jnp.bfloat16(head_scale)
    grad_key_low = grad_keys.reshape(token_count, local_width).astype(jnp.bfloat16)
    grad_value_low = grad_values.reshape(token_count, local_width).astype(jnp.bfloat16)
    grad_w_query = contract_rows(hidden, grad_query_pre)
    grad_b_query = jnp.sum(grad_query_pre.astype(jnp.float32), axis=0)
    grad_w_key = contract_rows(hidden, grad_key_low)
    grad_w_value = contract_rows(hidden, grad_value_low)
    grad_b_value = jnp.sum(grad_value_low.astype(jnp.float32), axis=0)
    input_part = (
        contract_cols(grad_query_pre, w_query)
        + contract_cols(grad_key_low, w_key)
        + contract_cols(grad_value_low, w_value)
    )
    gain_parts = jnp.stack([grad_gain_attn, grad_shift_attn, grad_gain_final, grad_shift_final])
    gain_term = jnp.where(lax.axis_index("mp") == 0, gain_parts, 0.0)
    hidden_sum, gain_sum = lax.psum((input_part, gain_term), "mp")
    grad_hidden = grad_one_part + hidden_sum
    every_sum = lax.psum(
        (
            grad_w_query,
            grad_b_query,
            grad_w_key,
            grad_w_value,
            grad_b_value,
            grad_w_out,
            grad_b_out,
            gain_sum,
            grad_w_inner,
            grad_b_inner,
            grad_w_outer,
            grad_b_outer,
            loss_term,
        ),
        "dp",
    )
    gains_done = every_sum[7]
    mean_loss = every_sum[12] / (dp_count * own_count)
    return (
        mean_loss.reshape(1),
        out_part,
        grad_hidden,
        every_sum[0],
        every_sum[1],
        every_sum[2],
        every_sum[3],
        every_sum[4],
        every_sum[5],
        every_sum[6],
        gains_done[0],
        gains_done[1],
        every_sum[8],
        every_sum[9],
        every_sum[10],
        every_sum[11],
        gains_done[2],
        gains_done[3],
    )


def solution(mesh):
    return jax.shard_map(
        on_device,
        mesh=mesh,
        in_specs=(
            P("dp", None),
            P("dp", None),
            P("dp"),
            P("dp", None),
            P(),
            P(None, "mp"),
            P("mp"),
            P(None, "mp"),
            P(None, "mp"),
            P("mp"),
            P("mp", None),
            P(),
            P(),
            P(),
            P(None, "mp"),
            P("mp"),
            P("mp", None),
            P(),
            P(),
            P(),
        ),
        out_specs=(
            P(),
            P("dp", None),
            P("dp", None),
            P(None, "mp"),
            P("mp"),
            P(None, "mp"),
            P(None, "mp"),
            P("mp"),
            P("mp", None),
            P(),
            P(),
            P(),
            P(None, "mp"),
            P("mp"),
            P("mp", None),
            P(),
            P(),
            P(),
        ),
        check_vma=False,
    )
```

profile of v0, /device:TPU:0, one launch (start us, length us, event | category | flops | bytes accessed | tf_op | source)
XLA Modules:
  0.0 1092.0 jit_solution(5726283432003561547)
XLA Ops:
  8.8 3.2 fusion.55
  12.7 3.2 fusion.56
  17.5 3.1 convolution_convert_fusion.1
  21.4 47.4 %while.32 = (s32[]{:T(128)}, bf16[4,512,3,64]{1,3,2,0:T(8,128)(2,1)}, f32[4,3,512,1]{2,1,3,0:T(4,128)}, s32[4]{0:T(128)S(1)}, bf16[2,1024,3,64]{1,3,2,0:T(8,128)...) while((s32[]{:T(128)}, ...), condition=%wide.region_3.4_spmd, body=%wide.region_0.3_spmd.sunk | while | flops 417430016 | bytes 22226292 | solution.py:121
  26.3 2.2 select_reduce_fusion.3
  30.7 2.6 fusion.143
  38.1 2.2 select_reduce_fusion.3
  42.5 2.6 fusion.143
  50.0 2.2 select_reduce_fusion.3
  54.4 2.6 fusion.143
  61.9 2.2 select_reduce_fusion.3
  66.2 2.6 fusion.143
  68.8 2.0 copy.48
  71.9 3.7 fusion.82
  75.9 122.2 %all-reduce.8.cloned.1.call-done = f32[2048,768]{1,0:T(8,128)} async-done(((f32[2048,768]{1,0:T(8,128)}), f32[2048,768]{1,0:T(8,128)}) %all-reduce.8.cloned.1.call-update) | async-done | bytes 6291472 | tf_op jit(solution)/shard_map/psum | solution.py:123
  198.1 4.6 fusion.80
  205.4 18.3 %multiply_convert_fusion.1 = (bf16[2048,768]{1,0:T(8,128)(2,1)S(1)}, f32[2048,768]{1,0:T(8,128)}, f32[2048,768]{1,0:T(8,128)}) fusion(f32[768]{0:T(1024)S(1)} %copy-done.48, bf16[2048,768]{1,0:T(8,128)(2,1)S(1)} %fusion.53, bf16[768,768]{1,0:T(8,128)(2,1)S(1)} %copy-done), kind=kOutput, calls=%fused_computation.81 | convolution fusion | flops 2519728128 | bytes 20057088 | tf_op jit(solution)/shard_map/dot_general | solution.py:130
  225.5 4.5 fusion.83
  231.0 118.9 %all-reduce.10.cloned.1.call-done = f32[2048,768]{1,0:T(8,128)} async-done(((f32[2048,768]{1,0:T(8,128)}), f32[2048,768]{1,0:T(8,128)}) %all-reduce.10.cloned.1.call-update) | async-done | bytes 6291472 | tf_op jit(solution)/shard_map/psum | solution.py:133
  349.9 5.7 fusion.78
  360.0 30.8 %all_gather.3 = bf16[128,768]{1,0:T(8,128)(2,1)S(1)} all-gather(bf16[16,768]{1,0:T(8,128)(2,1)S(1)} %slice.71), channel_id=1, replica_groups=mesh['dp'=8,'mp'=4] {'dp'}, dimensions={0}, use_global_device_ids=true | all-gather | bytes 221184 | tf_op jit(solution)/shard_map/all_gather | solution.py:156
  393.5 61.2 %reduce-scatter.2.cloned.1.call-done = f32[16,768]{1,0:T(8,128)} async-done(((f32[128,768]{1,0:T(8,128)}), f32[16,768]{1,0:T(8,128)}) %reduce-scatter.2.cloned.1.call-update) | async-done | bytes 49168 | tf_op jit(solution)/shard_map/reduce_scatter | solution.py:164
  454.7 8.7 multiply_reduce_fusion.1
  463.4 5.3 convert_reduce_fusion
  468.8 9.5 convert_reduce_fusion.1
  480.0 4.5 fusion.84
  485.0 118.3 %all-reduce.12.cloned.1.call-done = f32[2048,768]{1,0:T(8,128)} async-done(((f32[2048,768]{1,0:T(8,128)}), f32[2048,768]{1,0:T(8,128)}) %all-reduce.12.cloned.1.call-update) | async-done | bytes 6291472 | tf_op jit(solution)/shard_map/psum | solution.py:180
  603.3 8.7 multiply_reduce_fusion.2
  612.1 5.2 convert_reduce_fusion.2
  617.2 2.7 copy-done.3
  624.3 75.6 %while.33 = (s32[]{:T(128)}, f32[2,1024,192]{1,2,0:T(8,128)S(1)}, f32[2,1024,192]{1,2,0:T(8,128)}, bf16[4,512,192]{1,2,0:T(8,128)(2,1)}, s32[4]{0:T(128)S(1)}, /...) while((s32[]{:T(128)}, f32[2,1024,192]{1,2,0:T(8,128)S(1)}, ...), condition=%wide.region_24.25_spmd, body=%wide.region_21.24_spmd.sunk | while | flops 1026816512 | bytes 77071920 | solution.py:219
  628.8 2.1 fusion.152
  632.0 2.4 multiply_reduce_fusion.10
  647.7 2.1 fusion.152
  650.8 2.4 multiply_reduce_fusion.10
  666.5 2.1 fusion.152
  669.7 2.4 multiply_reduce_fusion.10
  685.4 2.1 fusion.152
  688.6 2.4 multiply_reduce_fusion.10
  705.3 3.7 add_add_fusion
  709.2 7.1 fusion.87
  716.2 7.1 fusion.70
  730.9 12.2 %psum.138 = f32[4,768]{1,0:T(4,128)S(1)} all-reduce(f32[4,768]{1,0:T(4,128)S(1)} %maximum_select_fusion), channel_id=1, replica_groups=mesh['dp'=8,'mp'=4] {'mp'}, use_global_device_ids=true, to_apply=%region_40.41 | all-reduce | flops 3072 | bytes 24576 | tf_op jit(solution)/shard_map/psum | solution.py:239
  744.5 37.9 %all-reduce = (f32[]{:T(128)}, f32[192]{0:T(256)}, f32[192]{0:T(256)}, f32[768]{0:T(1024)}, f32[4,768]{1,0:T(4,128)S(1)}, /*index=5*/f32[768]{0:T(1024)}, f32[768]{0:T(1024)}) all-reduce(f32[]{:T(128)} %subtract_reduce_fusion, f32[192]{0:T(256)S(1)} %convert_reduce_fusion.4, ...), channel_id=1, replica_groups=mesh['dp'=8,'mp'=4] {'dp'}, use_global_device_ids=true, to_apply=%region_14.15 | all-reduce | flops 5761 | bytes 46088 | tf_op jit(solution)/shard_map/psum | solution.py:241
  783.7 45.6 %all-reduce.14.cloned.1.call-done = f32[2048,768]{1,0:T(8,128)} async-done(((f32[2048,768]{1,0:T(8,128)}), f32[2048,768]{1,0:T(8,128)}) %all-reduce.14.cloned.1.call-update) | async-done | bytes 6291472 | tf_op jit(solution)/shard_map/psum | solution.py:239
  829.3 8.1 add.272
  837.4 235.7 %all-reduce.16.cloned.1.call-done = (f32[768,192]{0,1:T(8,128)}, f32[768,192]{0,1:T(8,128)}, f32[768,192]{0,1:T(8,128)}, f32[192,768]{1,0:T(8,128)}, f32[768,768]{1,0:T(8,128)}, /*index=5*/f32[768,768]{1,0:T(8,128)}) async-done(((f32[768,192]{0,1:T(8,128)}, f32[768,192]{0,1:T(8,128)}, f32[768,192]{0,1:T(8,128)}, f32[192,768]{1,0:T(8,128)}, f32[768,768]{1,0:T(8,128)}, /*index=5*/f32[768,768]{1,0:T(8,128)}), ...) | async-done | bytes 7077904 | tf_op jit(solution)/shard_map/psum | solution.py:241
  1073.1 2.1 copy.96
  (286 shorter events, 102.6 us)
Async XLA Ops:
  7.2 198.2 %copy-start = (bf16[768,768]{1,0:T(8,128)(2,1)S(1)}, bf16[768,768]{1,0:T(8,128)(2,1)}, u32[]{:S(2)}) copy-start(bf16[768,768]{1,0:T(8,128)(2,1)} %param.42) | copy-start | bytes 3538948
  7.2 190.9 %all-reduce.8.cloned.1.call-start = ((), (), s32[]{:S(2)}) async-start(), calls=%async_computation.1 | async-start | bytes 12582912 | tf_op jit(solution)/shard_map/psum | solution.py:123
  21.4 50.6 %copy-start.22 = (bf16[192,768]{1,0:T(8,128)(2,1)S(1)}, bf16[192,768]{1,0:T(8,128)(2,1)}, u32[]{:S(2)}) copy-start(bf16[192,768]{1,0:T(8,128)(2,1)} %param.38) | copy-start | bytes 884740
  68.8 6.9 copy-start.10
  71.9 126.2 %copy-start.43 = (f32[768]{0:T(1024)S(1)}, f32[768]{0:T(1024)}, u32[]{:S(2)}) copy-start(f32[768]{0:T(1024)} %param.39) | copy-start | bytes 9220
  75.7 274.2 %all-reduce.10.cloned.1.call-start = ((), (), s32[]{:S(2)}) async-start(), calls=%async_computation.2 | async-start | bytes 12582912 | tf_op jit(solution)/shard_map/psum | solution.py:133
  205.4 18.3 %copy-start.17 = (bf16[2048,768]{1,0:T(8,128)(2,1)}, bf16[2048,768]{1,0:T(8,128)(2,1)S(1)}, u32[]{:S(2)}) copy-start(bf16[2048,768]{1,0:T(8,128)(2,1)S(1)} %fusion.53) | copy-start | bytes 9437188
  205.4 20.1 %copy-start.46 = (bf16[768,768]{1,0:T(8,128)(2,1)S(1)}, bf16[768,768]{1,0:T(8,128)(2,1)}, u32[]{:S(2)}) copy-start(bf16[768,768]{1,0:T(8,128)(2,1)} %param.44) | copy-start | bytes 3538948
  230.0 120.0 %copy-start.44 = (f32[768]{0:T(1024)S(1)}, f32[768]{0:T(1024)}, u32[]{:S(2)}) copy-start(f32[768]{0:T(1024)} %param.45) | copy-start | bytes 9220
  230.0 224.7 %reduce-scatter.2.cloned.1.call-start = ((), (), s32[]{:S(2)}) async-start(), calls=%async_computation.3 | async-start | bytes 442368 | tf_op jit(solution)/shard_map/reduce_scatter | solution.py:164
  355.6 2.7 copy-start.4
  391.0 72.4 %copy-start.34 = (f32[16]{0:T(128)}, f32[16]{0:T(128)S(1)}, u32[]{:S(2)}) copy-start(f32[16]{0:T(128)S(1)} %get-tuple-element.447) | copy-start | bytes 196
  391.7 71.7 %copy-start.36 = (f32[16]{0:T(128)}, f32[16]{0:T(128)S(1)}, u32[]{:S(2)}) copy-start(f32[16]{0:T(128)S(1)} %get-tuple-element.368) | copy-start | bytes 196
  393.0 210.4 %all-reduce.12.cloned.1.call-start = ((), (), s32[]{:S(2)}) async-start(), calls=%async_computation.4 | async-start | bytes 12582912 | tf_op jit(solution)/shard_map/psum | solution.py:180
  454.7 14.1 %slice-start.2 = ((s8[6291456]{0:T(1024)(128)(4,1)}), s8[4194304]{0:T(1024)(128)(4,1)S(1)}, s32[]{:S(2)}) async-start(s8[6291456]{0:T(1024)(128)(4,1)} %bitcast.195), calls=%async_computation.9 | async-start | bytes 8388608
  463.4 5.4 copy-start.47
  463.4 5.4 slice-start.3
  468.8 9.5 copy-start.5
  484.6 344.7 %all-reduce.14.cloned.1.call-start = ((), (), s32[]{:S(2)}) async-start(), calls=%async_computation.5 | async-start | bytes 12582912 | tf_op jit(solution)/shard_map/psum | solution.py:239
  617.2 2.7 copy-start.3
  619.9 4.4 copy-start.33
  628.8 3.2 copy-start.11
  628.8 3.2 copy-start.14
  636.1 4.2 copy-start.7
  647.6 3.2 copy-start.11
  647.7 3.2 copy-start.14
  654.9 4.2 copy-start.7
  666.5 3.2 copy-start.11
  666.5 3.2 copy-start.14
  673.8 4.2 copy-start.7
  685.4 3.2 copy-start.11
  685.4 3.2 copy-start.14
  692.7 4.2 copy-start.7
  699.9 3.3 copy-start.23
  701.6 3.7 copy-start.15
  709.1 364.0 %all-reduce.16.cloned.1.call-start = ((), (), s32[]{:S(2)}) async-start(), calls=%async_computation.6 | async-start | bytes 14155776 | tf_op jit(solution)/shard_map/psum | solution.py:241
  709.2 7.1 copy-start.19
  716.2 7.1 copy-start.6
  716.2 7.1 copy-start.16
  723.4 5.0 slice-start
  723.4 5.0 copy-start.13
  725.0 3.3 slice-start.1
  728.4 16.1 %copy-start.30 = (f32[768]{0:T(1024)S(1)}, f32[768]{0:T(1024)}, u32[]{:S(2)}) copy-start(f32[768]{0:T(1024)} %get-tuple-element.425) | copy-start | bytes 9220
  728.4 16.1 %copy-start.31 = (f32[768]{0:T(1024)S(1)}, f32[768]{0:T(1024)}, u32[]{:S(2)}) copy-start(f32[768]{0:T(1024)} %get-tuple-element.427) | copy-start | bytes 9220
  728.5 16.1 %copy-start.42 = (f32[768]{0:T(1024)S(1)}, f32[768]{0:T(1024)}, u32[]{:S(2)}) copy-start(f32[768]{0:T(1024)} %get-tuple-element.450) | copy-start | bytes 9220
  1073.1 7.9 copy-start.21
  1073.1 9.3 copy-start.20
  1073.1 10.7 copy-start.1
  (25 other events, 37.5 us)
Sparse Core Ops, SparseCore 0:
  75.8 122.2 all-reduce.7
  230.1 119.7 all-reduce.9
  393.1 61.5 reduce-scatter.1
  484.7 118.5 all-reduce.11
  709.2 120.0 all-reduce.13
  835.4 237.6 all-reduce.15
where the time goes:
time: 1100 us; the launch traced here: 1090 us
  waiting for transfers between devices  702 us (64%)
  matrix products  144 us (13%)
  blocking collectives  80.9 us (7%)
  other arithmetic  73 us (7%)
  local copies, waits for them, and re-layouts  42.4 us (4%)
  loops' own time  31.8 us (3%)
  between operations  16.8 us (2%)
    psum x1, waiting for transfers between devices, on_device(): lax.psum((grad_w_query, grad_b_query, grad_w_key, grad_w_value, grad_b_va...  236 us
    psum x1, waiting for transfers between devices, on_device(): lax.psum(jnp.dot(context, w_out, preferred_element_type=jnp.float32), 'mp')  122 us
    psum x1, waiting for transfers between devices, on_device(): lax.psum(jnp.dot(inner_act, w_outer, preferred_element_type=jnp.float32),...  119 us
    psum x1, waiting for transfers between devices, on_device(): back_part = lax.psum(contract_cols(grad_pre, w_inner), 'mp')  118 us
    reduce_scatter x1, waiting for transfers between devices, on_device(): lax.psum_scatter(passage_terms, 'dp', scatter_dimension=0, tiled=True)  61.2 us
    psum x1, waiting for transfers between devices, on_device(): hidden_sum, gain_sum = lax.psum((input_part, gain_term), 'mp')  45.6 us
    psum x1, blocking collectives, on_device(): lax.psum((grad_w_query, grad_b_query, grad_w_key, grad_w_value, grad_b_va...  37.9 us
    all_gather x1, blocking collectives, on_device(): passage_all = lax.all_gather(passage_vecs, 'dp', axis=0, tiled=True)  30.8 us
  transfers between devices with their start and end apart: 6, of which 6 were waited for; matrix products, arithmetic and copies ran while one was open for 3% of the time, Pallas kernels for 0%

commit v1 on v0

--- a/solution.py
+++ b/solution.py
@@ -130,7 +130,10 @@
     pre_act = jnp.dot(middle_low_part, w_inner, preferred_element_type=jnp.float32) + b_inner
     activated, gelu_back = jax.vjp(partial(jax.nn.gelu, approximate=False), pre_act)
     inner_act = activated.astype(jnp.bfloat16)
-    feed_part = lax.psum(jnp.dot(inner_act, w_outer, preferred_element_type=jnp.float32), "mp")
+    feed_part = jnp.sum(
+        lax.all_gather(jnp.dot(inner_act, w_outer, preferred_element_type=jnp.float32), "mp"),
+        axis=0,
+    )
     feed_part = feed_part + b_outer
     final_part, normed_two, inverse_two = norm_forward(
         middle_part + feed_part, gain_final, shift_final

time: 1100 us -> 1150 us (1.045)
  waiting for transfers between devices: 702 us -> 737 us
  other arithmetic: 73 us -> 85.7 us
    all_gather x0 -> x1, waiting for transfers between devices: none -> 154 us  [on_device(): lax.all_gather(jnp.dot(inner_act, w_outer, preferred_element_type=jnp.flo...]
    psum x1 -> x0, waiting for transfers between devices: 119 us -> none  [on_device(): lax.psum(jnp.dot(inner_act, w_outer, preferred_element_type=jnp.float32),...]
    reduce_sum x0 -> x1, other arithmetic: none -> 12.6 us  [on_device(): jnp.sum(lax.all_gather(jnp.dot(inner_act, w_outer, preferred_element_type...]
where the time goes in v1:
time: 1150 us; the launch traced here: 1140 us
  waiting for transfers between devices  737 us (64%)
  matrix products  144 us (13%)
  other arithmetic  85.7 us (7%)
  blocking collectives  80.8 us (7%)
  local copies, waits for them, and re-layouts  42.3 us (4%)
  loops' own time  31.8 us (3%)
  between operations  16.8 us (1%)
    psum x1, waiting for transfers between devices, on_device(): lax.psum((grad_w_query, grad_b_query, grad_w_key, grad_w_value, grad_b_va...  236 us
    all_gather x1, waiting for transfers between devices, on_device(): lax.all_gather(jnp.dot(inner_act, w_outer, preferred_element_type=jnp.flo...  154 us
    psum x1, waiting for transfers between devices, on_device(): lax.psum(jnp.dot(context, w_out, preferred_element_type=jnp.float32), 'mp')  122 us
    psum x1, waiting for transfers between devices, on_device(): back_part = lax.psum(contract_cols(grad_pre, w_inner), 'mp')  118 us
    reduce_scatter x1, waiting for transfers between devices, on_device(): lax.psum_scatter(passage_terms, 'dp', scatter_dimension=0, tiled=True)  61 us
    psum x1, waiting for transfers between devices, on_device(): hidden_sum, gain_sum = lax.psum((input_part, gain_term), 'mp')  45.6 us
    psum x1, blocking collectives, on_device(): lax.psum((grad_w_query, grad_b_query, grad_w_key, grad_w_value, grad_b_va...  37.9 us
    all_gather x1, blocking collectives, on_device(): passage_all = lax.all_gather(passage_vecs, 'dp', axis=0, tiled=True)  30.7 us
  transfers between devices with their start and end apart: 6, of which 6 were waited for; matrix products, arithmetic and copies ran while one was open for 3% of the time, Pallas kernels for 0%

profile of v1, /device:TPU:0, one launch (start us, length us, event | category | flops | bytes accessed | tf_op | source)
XLA Modules:
  0.0 1139.5 jit_solution(14359836886609176762)
XLA Ops:
  8.8 3.2 fusion.55
  12.7 3.2 fusion.56
  17.5 3.1 convolution_convert_fusion.1
  21.4 47.4 %while.32 = (s32[]{:T(128)}, bf16[4,512,3,64]{1,3,2,0:T(8,128)(2,1)}, f32[4,3,512,1]{2,1,3,0:T(4,128)}, s32[4]{0:T(128)S(1)}, bf16[2,1024,3,64]{1,3,2,0:T(8,128)...) while((s32[]{:T(128)}, ...), condition=%wide.region_3.4_spmd, body=%wide.region_0.3_spmd.sunk | while | flops 417430016 | bytes 22226292 | solution.py:121
  26.3 2.2 select_reduce_fusion.3
  30.7 2.6 fusion.143
  38.1 2.2 select_reduce_fusion.3
  42.5 2.6 fusion.143
  50.0 2.2 select_reduce_fusion.3
  54.4 2.6 fusion.143
  61.9 2.2 select_reduce_fusion.3
  66.2 2.6 fusion.143
  71.9 3.7 fusion.82
  75.9 122.2 %all-reduce.7.cloned.1.call-done = f32[2048,768]{1,0:T(8,128)} async-done(((f32[2048,768]{1,0:T(8,128)}), f32[2048,768]{1,0:T(8,128)}) %all-reduce.7.cloned.1.call-update) | async-done | bytes 6291472 | tf_op jit(solution)/shard_map/psum | solution.py:123
  198.1 4.6 fusion.80
  205.5 18.3 %multiply_convert_fusion.1 = (bf16[2048,768]{1,0:T(8,128)(2,1)S(1)}, f32[2048,768]{1,0:T(8,128)}, f32[2048,768]{1,0:T(8,128)}) fusion(f32[768]{0:T(1024)S(1)} %copy-done.48, bf16[2048,768]{1,0:T(8,128)(2,1)S(1)} %fusion.53, bf16[768,768]{1,0:T(8,128)(2,1)S(1)} %copy-done), kind=kOutput, calls=%fused_computation.81 | convolution fusion | flops 2519728128 | bytes 20057088 | tf_op jit(solution)/shard_map/dot_general | solution.py:130
  225.5 4.5 fusion.83
  231.0 154.2 %all-gather.3.cloned.1.call-done = f32[8192,768]{1,0:T(8,128)} async-done(((f32[2048,768]{1,0:T(8,128)}), f32[8192,768]{1,0:T(8,128)}) %all-gather.3.cloned.1.call-update) | async-done | bytes 25165840 | tf_op jit(solution)/shard_map/all_gather | solution.py:134
  385.2 12.6 %reduce_sum.215 = f32[2048,768]{1,0:T(8,128)} reduce(f32[4,2048,768]{2,1,0:T(8,128)} %bitcast.182, f32[]{:T(128)} %constant.234.clone.1), dimensions={0}, to_apply=%region_7.8 | reduce | flops 4718592 | bytes 31457284 | tf_op jit(solution)/shard_map/reduce_sum | solution.py:133
  397.8 5.7 fusion.78
  407.9 30.7 %all_gather.11 = bf16[128,768]{1,0:T(8,128)(2,1)S(1)} all-gather(bf16[16,768]{1,0:T(8,128)(2,1)S(1)} %slice.71), channel_id=1, replica_groups=mesh['dp'=8,'mp'=4] {'dp'}, dimensions={0}, use_global_device_ids=true | all-gather | bytes 221184 | tf_op jit(solution)/shard_map/all_gather | solution.py:159
  441.3 61.0 %reduce-scatter.2.cloned.1.call-done = f32[16,768]{1,0:T(8,128)} async-done(((f32[128,768]{1,0:T(8,128)}), f32[16,768]{1,0:T(8,128)}) %reduce-scatter.2.cloned.1.call-update) | async-done | bytes 49168 | tf_op jit(solution)/shard_map/reduce_scatter | solution.py:167
  502.3 8.7 multiply_reduce_fusion.1
  511.0 5.3 convert_reduce_fusion
  516.4 9.5 convert_reduce_fusion.1
  527.6 4.5 fusion.84
  532.6 118.3 %all-reduce.9.cloned.1.call-done = f32[2048,768]{1,0:T(8,128)} async-done(((f32[2048,768]{1,0:T(8,128)}), f32[2048,768]{1,0:T(8,128)}) %all-reduce.9.cloned.1.call-update) | async-done | bytes 6291472 | tf_op jit(solution)/shard_map/psum | solution.py:183
  650.9 8.7 multiply_reduce_fusion.2
  659.7 5.2 convert_reduce_fusion.2
  664.8 2.7 copy-done.3
  671.9 75.6 %while.33 = (s32[]{:T(128)}, f32[2,1024,192]{1,2,0:T(8,128)S(1)}, f32[2,1024,192]{1,2,0:T(8,128)}, bf16[4,512,192]{1,2,0:T(8,128)(2,1)}, s32[4]{0:T(128)S(1)}, /...) while((s32[]{:T(128)}, f32[2,1024,192]{1,2,0:T(8,128)S(1)}, ...), condition=%wide.region_24.25_spmd, body=%wide.region_21.24_spmd.sunk | while | flops 1026816512 | bytes 77071920 | solution.py:222
  676.4 2.1 fusion.152
  679.5 2.4 multiply_reduce_fusion.10
  695.2 2.1 fusion.152
  698.4 2.4 multiply_reduce_fusion.10
  714.1 2.1 fusion.152
  717.3 2.4 multiply_reduce_fusion.10
  732.9 2.1 fusion.152
  736.1 2.4 multiply_reduce_fusion.10
  752.9 3.7 add_add_fusion
  756.7 7.1 fusion.87
  763.8 7.1 fusion.70
  778.4 12.3 %psum.130 = f32[4,768]{1,0:T(4,128)S(1)} all-reduce(f32[4,768]{1,0:T(4,128)S(1)} %maximum_select_fusion), channel_id=1, replica_groups=mesh['dp'=8,'mp'=4] {'mp'}, use_global_device_ids=true, to_apply=%region_40.41 | all-reduce | flops 3072 | bytes 24576 | tf_op jit(solution)/shard_map/psum | solution.py:242
  792.1 37.9 %all-reduce = (f32[]{:T(128)}, f32[192]{0:T(256)}, f32[192]{0:T(256)}, f32[768]{0:T(1024)}, f32[4,768]{1,0:T(4,128)S(1)}, /*index=5*/f32[768]{0:T(1024)}, f32[768]{0:T(1024)}) all-reduce(f32[]{:T(128)} %subtract_reduce_fusion, f32[192]{0:T(256)S(1)} %convert_reduce_fusion.4, ...), channel_id=1, replica_groups=mesh['dp'=8,'mp'=4] {'dp'}, use_global_device_ids=true, to_apply=%region_14.15 | all-reduce | flops 5761 | bytes 46088 | tf_op jit(solution)/shard_map/psum | solution.py:244
  831.3 45.6 %all-reduce.11.cloned.1.call-done = f32[2048,768]{1,0:T(8,128)} async-done(((f32[2048,768]{1,0:T(8,128)}), f32[2048,768]{1,0:T(8,128)}) %all-reduce.11.cloned.1.call-update) | async-done | bytes 6291472 | tf_op jit(solution)/shard_map/psum | solution.py:242
  876.9 8.1 add.270
  885.0 235.6 %all-reduce.13.cloned.1.call-done = (f32[768,192]{0,1:T(8,128)}, f32[768,192]{0,1:T(8,128)}, f32[768,192]{0,1:T(8,128)}, f32[192,768]{1,0:T(8,128)}, f32[768,768]{1,0:T(8,128)}, /*index=5*/f32[768,768]{1,0:T(8,128)}) async-done(((f32[768,192]{0,1:T(8,128)}, f32[768,192]{0,1:T(8,128)}, f32[768,192]{0,1:T(8,128)}, f32[192,768]{1,0:T(8,128)}, f32[768,768]{1,0:T(8,128)}, /*index=5*/f32[768,768]{1,0:T(8,128)}), ...) | async-done | bytes 7077904 | tf_op jit(solution)/shard_map/psum | solution.py:244
  1120.6 2.1 copy.96
  (287 shorter events, 104.6 us)
Async XLA Ops:
  7.2 198.3 %copy-start = (bf16[768,768]{1,0:T(8,128)(2,1)S(1)}, bf16[768,768]{1,0:T(8,128)(2,1)}, u32[]{:S(2)}) copy-start(bf16[768,768]{1,0:T(8,128)(2,1)} %param.42) | copy-start | bytes 3538948
  7.2 190.9 %all-reduce.7.cloned.1.call-start = ((), (), s32[]{:S(2)}) async-start(), calls=%async_computation.1 | async-start | bytes 12582912 | tf_op jit(solution)/shard_map/psum | solution.py:123
  21.4 50.6 %copy-start.22 = (bf16[192,768]{1,0:T(8,128)(2,1)S(1)}, bf16[192,768]{1,0:T(8,128)(2,1)}, u32[]{:S(2)}) copy-start(bf16[192,768]{1,0:T(8,128)(2,1)} %param.38) | copy-start | bytes 884740
  68.8 6.9 copy-start.10
  71.9 126.2 %copy-start.43 = (f32[768]{0:T(1024)S(1)}, f32[768]{0:T(1024)}, u32[]{:S(2)}) copy-start(f32[768]{0:T(1024)} %param.39) | copy-start | bytes 9220
  75.7 309.5 %all-gather.3.cloned.1.call-start = ((), (), s32[]{:S(2)}) async-start(), calls=%async_computation.5 | async-start | bytes 31457280 | tf_op jit(solution)/shard_map/all_gather | solution.py:134
  202.8 2.7 copy-start.2
  205.5 18.3 %copy-start.17 = (bf16[2048,768]{1,0:T(8,128)(2,1)}, bf16[2048,768]{1,0:T(8,128)(2,1)S(1)}, u32[]{:S(2)}) copy-start(bf16[2048,768]{1,0:T(8,128)(2,1)S(1)} %fusion.53) | copy-start | bytes 9437188
  205.5 20.0 %copy-start.46 = (bf16[768,768]{1,0:T(8,128)(2,1)S(1)}, bf16[768,768]{1,0:T(8,128)(2,1)}, u32[]{:S(2)}) copy-start(bf16[768,768]{1,0:T(8,128)(2,1)} %param.44) | copy-start | bytes 3538948
  230.0 272.3 %reduce-scatter.2.cloned.1.call-start = ((), (), s32[]{:S(2)}) async-start(), calls=%async_computation.2 | async-start | bytes 442368 | tf_op jit(solution)/shard_map/reduce_scatter | solution.py:167
  385.2 12.6 %copy-start.44 = (f32[768]{0:T(1024)S(1)}, f32[768]{0:T(1024)}, u32[]{:S(2)}) copy-start(f32[768]{0:T(1024)} %param.45) | copy-start | bytes 9220
  438.8 72.2 %copy-start.34 = (f32[16]{0:T(128)}, f32[16]{0:T(128)S(1)}, u32[]{:S(2)}) copy-start(f32[16]{0:T(128)S(1)} %get-tuple-element.447) | copy-start | bytes 196
  439.5 71.4 %copy-start.36 = (f32[16]{0:T(128)}, f32[16]{0:T(128)S(1)}, u32[]{:S(2)}) copy-start(f32[16]{0:T(128)S(1)} %get-tuple-element.368) | copy-start | bytes 196
  440.8 210.2 %all-reduce.9.cloned.1.call-start = ((), (), s32[]{:S(2)}) async-start(), calls=%async_computation.3 | async-start | bytes 12582912 | tf_op jit(solution)/shard_map/psum | solution.py:183
  502.3 14.1 %slice-start.2 = ((s8[6291456]{0:T(1024)(128)(4,1)}), s8[4194304]{0:T(1024)(128)(4,1)S(1)}, s32[]{:S(2)}) async-start(s8[6291456]{0:T(1024)(128)(4,1)} %bitcast.197), calls=%async_computation.9 | async-start | bytes 8388608
  511.0 5.4 copy-start.47
  511.0 5.4 slice-start.3
  516.3 9.5 copy-start.5
  532.1 344.8 %all-reduce.11.cloned.1.call-start = ((), (), s32[]{:S(2)}) async-start(), calls=%async_computation.4 | async-start | bytes 12582912 | tf_op jit(solution)/shard_map/psum | solution.py:242
  664.8 2.7 copy-start.3
  667.5 4.3 copy-start.33
  676.3 3.2 copy-start.11
  676.4 3.2 copy-start.14
  683.6 4.2 copy-start.7
  695.2 3.2 copy-start.11
  695.2 3.2 copy-start.14
  702.5 4.2 copy-start.7
  714.1 3.2 copy-start.11
  714.1 3.2 copy-start.14
  721.4 4.2 copy-start.7
  732.9 3.2 copy-start.11
  732.9 3.2 copy-start.14
  740.2 4.2 copy-start.7
  747.4 3.3 copy-start.23
  749.2 3.7 copy-start.15
  756.7 364.0 %all-reduce.13.cloned.1.call-start = ((), (), s32[]{:S(2)}) async-start(), calls=%async_computation.6 | async-start | bytes 14155776 | tf_op jit(solution)/shard_map/psum | solution.py:244
  756.7 7.1 copy-start.19
  763.8 7.1 copy-start.6
  763.8 7.1 copy-start.16
  770.9 5.0 slice-start
  770.9 5.0 copy-start.13
  772.6 3.3 slice-start.1
  776.0 16.1 %copy-start.30 = (f32[768]{0:T(1024)S(1)}, f32[768]{0:T(1024)}, u32[]{:S(2)}) copy-start(f32[768]{0:T(1024)} %get-tuple-element.425) | copy-start | bytes 9220
  776.0 16.1 %copy-start.31 = (f32[768]{0:T(1024)S(1)}, f32[768]{0:T(1024)}, u32[]{:S(2)}) copy-start(f32[768]{0:T(1024)} %get-tuple-element.427) | copy-start | bytes 9220
  776.0 16.1 %copy-start.42 = (f32[768]{0:T(1024)S(1)}, f32[768]{0:T(1024)}, u32[]{:S(2)}) copy-start(f32[768]{0:T(1024)} %get-tuple-element.450) | copy-start | bytes 9220
  1120.6 7.9 copy-start.21
  1120.6 9.3 copy-start.20
  1120.6 10.7 copy-start.1
  (25 other events, 37.5 us)
Sparse Core Ops, SparseCore 0:
  75.8 122.2 all-reduce.6
  230.1 155.0 all-gather.2
  440.9 61.3 reduce-scatter.1
  532.3 118.6 all-reduce.8
  756.8 120.0 all-reduce.10
  883.0 237.6 all-reduce.12
